TPU v7x, 32 devices: a whole 2x2x4 slice. The times are simulated.
32 devices in a mesh: dom: 16 (over z, x, core), feat: 2 (over y).
Axes of the slice: x: 2, y: 2, z: 4, core: 2. Of those that a mesh axis runs over, the one named last changes fastest.
Arguments:
- features: bfloat16 [65536, 1024], P('dom', 'feat'), may hold values from -6 to 6
- w_self: bfloat16 [1024, 256], P('feat'), may hold values from -0.1875 to 0.1875
- w_neigh: bfloat16 [1024, 256], P('feat'), may hold values from -0.1875 to 0.1875
- hidden_bias: float32 [256], replicated, may hold values from -3 to 3
- edge_tiles: bfloat16 [16, 102, 128, 128], P('dom'), may hold values from 0 to 0.099609375
- tile_dst: int32 [16, 102], P('dom'), may hold values from 0 to 31, as said below
- tile_src: int32 [16, 102], P('dom'), may hold values from 0 to 47, as said below
- tile_count: int32 [16], P('dom'), may hold values from 12 to 102, as said below
- bound_rows: int32 [16, 256], P('dom'), may hold values from 0 to 4095, as said below
- send_pick: int32 [16, 16, 128], P('dom'), may hold values from 0 to 255, as said below
- cotangent: bfloat16 [65536, 256], P(('dom', 'feat')), may hold values from -0.0234375 to 0.0234375
Outputs:
- hidden: bfloat16 [65536, 256], P(('dom', 'feat'))
- grad_self: bfloat16 [1024, 256], P('feat')
- grad_neigh: bfloat16 [1024, 256], P('feat')
- grad_bias: float32 [256], replicated
Inputs may be any that keep to these rules, and one draw needn't show every extreme that they name: Within a partition the pairs (tile_dst, tile_src) of its 102 slots are distinct. `tile_src`: A source block below 32 is a row tile of the partition itself; block 32 + q is the block received from partition q. Slots from tile_count[p] on are unused. Some partition uses all 102 slots. `bound_rows`: distinct within each partition. Each list send_pick[p, q] has no repeats.
All inputs are finite; a program needn't handle non-finite values.
Results may differ from a plain program's by a relative error of at most 0.009.
The roundings to bfloat16 on the way count: a program that leaves them out, or rounds other values in their place, can miss the bound.
Values may be sent and summed in bfloat16 or wider, within the bound.
A program may use at most 128 MiB of HBM per device.

v0:
```python
import functools

import jax
import jax.numpy as jnp
from jax import lax
from jax.experimental import pallas as pl
from jax.experimental.pallas import tpu as pltpu
from jax.sharding import PartitionSpec as P

LEVELS = 32767.0
TINY = 1e-30
AHEAD = 4
LAG = 3
MESH = pl.DeviceIdType.MESH
F32 = jnp.float32
BF16 = jnp.bfloat16
VMEM = pl.BlockSpec(memory_space=pltpu.VMEM)
SMEM = pl.BlockSpec(memory_space=pltpu.SMEM)
TN = (((0,), (0,)), ((), ()))


def boundary_kernel(n, feat_ref, bound_ref, pick_ref, out_ref, blocks, send, recv, side_send, side_recv, local):
    chips = n // 2
    turn = chips // 2
    full = chips // 2 - 1
    ub = bound_ref.shape[1]
    width = feat_ref.shape[1]
    pick = pick_ref.shape[1]
    half_rows = ub // 2
    parts = ((0, half_rows), (half_rows, ub - half_rows + n))

    me = lax.axis_index("dom")
    core = me % 2
    chip = me // 2
    col = chip % 2
    row = chip // 2
    place = (1 - col) * row + col * (chips - 1 - row)

    def dom_of(position, which):
        position = (position + 2 * chips) % chips
        up = position // turn
        at = (1 - up) * 2 * position + up * (2 * (chips - 1 - position) + 1)
        return at * 2 + which

    ahead = dom_of(place + 1, core)
    behind = dom_of(place - 1, core)
    sibling = me + 1 - 2 * core

    barrier = pltpu.get_barrier_semaphore()
    for other in (ahead, behind, sibling):
        pl.semaphore_signal(barrier, inc=1, device_id={"dom": other}, device_id_type=MESH)

    nodes = feat_ref.shape[0]
    kept = pltpu.make_async_copy(feat_ref, out_ref.at[pl.ds(0, nodes)], local.at[0])
    kept.start()
    depth = min(512, nodes)
    wanted = bound_ref[0:1, :]

    def add_rows(k, total):
        ids = lax.broadcasted_iota(jnp.int32, (depth, ub), 0) + k * depth
        hot = jnp.where(ids == wanted, 1.0, 0.0).astype(BF16)
        rows = feat_ref[pl.ds(pl.multiple_of(k * depth, depth), depth), :]
        return total + lax.dot_general(hot, rows, TN, preferred_element_type=F32)

    total = lax.fori_loop(0, nodes // depth, add_rows, jnp.zeros((ub, width), F32))
    blocks[me, 0:ub, :] = total.astype(BF16)
    blocks[me, ub : ub + n, 0:pick] = pick_ref[...]
    if width > pick:
        blocks[me, ub : ub + n, pick:width] = jnp.zeros((n, width - pick), BF16)
    pl.semaphore_wait(barrier, 3)

    def hop(way, step, h):
        source = place - step if way == 0 else place + step
        owner = dom_of(source, core)
        at = blocks.at[owner, pl.ds(parts[h][0], parts[h][1])]
        return pltpu.make_async_remote_copy(
            src_ref=at,
            dst_ref=at,
            send_sem=send.at[way, step, h],
            recv_sem=recv.at[way, step, h],
            device_id={"dom": ahead if way == 0 else behind},
            device_id_type=MESH,
        )

    def aside(i, owner):
        return pltpu.make_async_remote_copy(
            src_ref=blocks.at[owner],
            dst_ref=blocks.at[owner],
            send_sem=side_send.at[i],
            recv_sem=side_recv.at[i],
            device_id={"dom": sibling},
            device_id_type=MESH,
        )

    def take(owner):
        table = blocks[owner, ub : ub + n, 0:pick].astype(F32)
        rows = lax.broadcasted_iota(jnp.int32, (n, pick), 0)
        mine = jnp.sum(jnp.where(rows == me, table, 0.0), axis=0, keepdims=True)
        ids = lax.broadcasted_iota(jnp.int32, (ub, pick), 0).astype(F32)
        hot = jnp.where(ids == mine, 1.0, 0.0).astype(BF16)
        got = lax.dot_general(hot, blocks[owner, 0:ub, :], TN, preferred_element_type=F32)
        at = pl.ds(pl.multiple_of(nodes + owner * pick, pick), pick)
        out_ref[at, :] = got.astype(BF16)

    started = []
    sides = []
    side_seen = 0

    def arrived(position):
        i = len(sides)
        copy = aside(i, dom_of(position, core))
        copy.start()
        sides.append((copy, position))

    for step in range(full + 1):
        for h in (0, 1):
            for way in (0, 1):
                if step > 0:
                    hop(way, step - 1, h).wait_recv()
                if step < full or h == way:
                    copy = hop(way, step, h)
                    copy.start()
                    started.append(copy)
        if step == 0:
            arrived(place)
            take(me)
        else:
            for position in (place - step, place + step):
                arrived(position)
                take(dom_of(position, core))
            while side_seen < len(sides) - 2:
                copy, position = sides[side_seen]
                copy.wait_recv()
                take(dom_of(position, 1 - core))
                side_seen += 1
    hop(0, full, 0).wait_recv()
    hop(1, full, 1).wait_recv()
    arrived(place + full + 1)
    take(dom_of(place + full + 1, core))
    while side_seen < len(sides):
        copy, position = sides[side_seen]
        copy.wait_recv()
        take(dom_of(position, 1 - core))
        side_seen += 1
    for copy in started:
        copy.wait_send()
    for copy, _ in sides:
        copy.wait_send()
    kept.wait()


def source_rows(n, features, bound_rows, send_pick):
    width = features.shape[1]
    ub = bound_rows.shape[1]
    pick = send_pick.shape[1]
    steps = n // 4
    return pl.pallas_call(
        functools.partial(boundary_kernel, n),
        out_shape=jax.ShapeDtypeStruct((features.shape[0] + n * pick, width), BF16),
        in_specs=[VMEM] * 3,
        out_specs=VMEM,
        scratch_shapes=[
            pltpu.VMEM((n, ub + n, width), BF16),
            pltpu.SemaphoreType.DMA((2, steps, 2)),
            pltpu.SemaphoreType.DMA((2, steps, 2)),
            pltpu.SemaphoreType.DMA((n // 2,)),
            pltpu.SemaphoreType.DMA((n // 2,)),
            pltpu.SemaphoreType.DMA((1,)),
        ],
        compiler_params=pltpu.CompilerParams(
            collective_id=0, has_side_effects=True, vmem_limit_bytes=40 * 2**20
        ),
    )(features, bound_rows, send_pick.astype(BF16))


def tile_kernel(group, dst_ref, src_ref, count_ref, source_ref, tiles_ref, out_ref, total):
    tile = tiles_ref.shape[1]
    total[...] = jnp.zeros_like(total)
    count = count_ref[0]

    def slots(g, carry):
        products = []
        for u in range(group):
            e = g * group + u
            block = source_ref[pl.ds(pl.multiple_of(src_ref[0, e] * tile, tile), tile), :]
            product = jnp.dot(tiles_ref[e], block, preferred_element_type=F32)
            products.append(jnp.where(e < count, product, 0.0))
        for u in range(group):
            e = g * group + u
            at = pl.ds(pl.multiple_of(dst_ref[0, e] * tile, tile), tile)
            total[at, :] += products[u]
        return carry

    lax.fori_loop(0, (count + group - 1) // group, slots, 0)
    out_ref[...] = total[...].astype(BF16)


def aggregate(nodes, source, edge_tiles, tile_dst, tile_src, tile_count):
    width = source.shape[1]
    slots = edge_tiles.shape[0]
    group = next(g for g in (3, 2, 1) if slots % g == 0)
    return pl.pallas_call(
        functools.partial(tile_kernel, group),
        out_shape=jax.ShapeDtypeStruct((nodes, width), BF16),
        in_specs=[SMEM, SMEM, SMEM, VMEM, VMEM],
        out_specs=VMEM,
        scratch_shapes=[pltpu.VMEM((nodes, width), F32)],
        compiler_params=pltpu.CompilerParams(vmem_limit_bytes=30 * 2**20),
    )(tile_dst, tile_src, tile_count, source, edge_tiles)


def halving_plan(n, rows):
    plan = []
    length = rows
    bit = 1
    while bit < n:
        halve = length % 32 == 0
        if halve:
            length //= 2
        plan.append((bit, halve, length))
        bit *= 2
    return plan


def layer_kernel(
    n, nf, plan, chunk, waves,
    feat_ref, agg_ref, ws_ref, wn_ref, bias_ref, cot_ref,
    hidden_ref, gs_ref, gn_ref, gb_ref,
    outgoing, incoming, scales, grads, total, sums, result, halves, small,
    psend, precv, ssend, srecv, gsend, grecv, hsend, hrecv, bsend, brecv, asend, arecv,
):
    me = lax.axis_index("dom")
    f = lax.axis_index("feat")
    owned, units = cot_ref.shape
    width = feat_ref.shape[1]
    chunks = owned // chunk
    lanes = units // waves
    items = waves * chunks
    ahead = min(AHEAD, items)
    lag = min(LAG, chunks)
    span = chunk // 8
    partners = []
    for bit, _, _ in plan:
        side = (me // bit) % 2
        partners.append((me + bit - 2 * bit * side, side))
    peers = [(f + k) % nf for k in range(1, nf)]

    barrier = pltpu.get_barrier_semaphore()
    for peer in peers:
        pl.semaphore_signal(barrier, inc=1, device_id={"feat": peer}, device_id_type=MESH)
    for partner, _ in partners:
        pl.semaphore_signal(barrier, inc=1, device_id={"dom": partner}, device_id_type=MESH)
    total[...] = jnp.zeros_like(total)
    pl.semaphore_wait(barrier, nf - 1 + len(plan))

    def at_rows(owner, j):
        return pl.ds(pl.multiple_of(owner * owned + j * chunk, chunk), chunk)

    def at_units(w):
        return pl.ds(pl.multiple_of(w * lanes, lanes), lanes)

    def inside(j):
        return pl.ds(pl.multiple_of(j * chunk, chunk), chunk)

    def partial(owner, j, w):
        rows = at_rows(owner, j)
        cols = at_units(w)
        return jnp.dot(feat_ref[rows, :], ws_ref[:, cols], preferred_element_type=F32) + jnp.dot(
            agg_ref[rows, :], wn_ref[:, cols], preferred_element_type=F32
        )

    def push(src, dst, send_sem, recv_sem, axis, to):
        return pltpu.make_async_remote_copy(
            src_ref=src,
            dst_ref=dst,
            send_sem=send_sem,
            recv_sem=recv_sem,
            device_id={axis: to},
            device_id_type=MESH,
        )

    def partial_copy(k, i):
        return push(
            outgoing.at[k, i], incoming.at[k, i], psend.at[k, i], precv.at[k, i], "feat", peers[k]
        )

    def scale_copy(k, i):
        return push(
            scales.at[0, k, i], scales.at[1, k, i], ssend.at[k, i], srecv.at[k, i], "feat", peers[k]
        )

    def grad_copy(k, i):
        at = grads.at[i // chunks, at_rows(f, i % chunks)]
        return push(at, at, gsend.at[k, i], grecv.at[k, i], "feat", peers[k])

    def send_partial(i):
        w, j = i // chunks, i % chunks
        for k in range(nf - 1):
            value = partial(peers[k], j, w).reshape(8, span, lanes)
            top = jnp.max(jnp.max(jnp.abs(value), axis=1), axis=1, keepdims=True)
            top = jnp.broadcast_to(jnp.maximum(top, TINY), (8, lanes))
            scales[0, k, i] = top * (1.0 / LEVELS)
            steps = jnp.round(value * (LEVELS / top)[:, None, :])
            steps = steps.reshape(chunk, lanes).astype(jnp.int32)
            outgoing[k, i] = steps.astype(jnp.int16)
            scale_copy(k, i).start()
            partial_copy(k, i).start()

    def add_grads(owner, i):
        w, j = i // chunks, i % chunks
        rows = at_rows(owner, j)
        block = grads[w, rows, :]
        total[w, 0:width, :] += lax.dot_general(
            feat_ref[rows, :], block, TN, preferred_element_type=F32
        )
        total[w, width : 2 * width, :] += lax.dot_general(
            agg_ref[rows, :], block, TN, preferred_element_type=F32
        )
        wide = block.astype(F32).reshape(chunk // 8, 8, lanes)
        sums[w, owner * chunks + j] = jnp.sum(wide, axis=0)

    def finish(i):
        w, j = i // chunks, i % chunks
        preact = partial(f, j, w)
        cols = at_units(w)
        for k in range(nf - 1):
            scale_copy(k, i).wait_recv()
            partial_copy(k, i).wait_recv()
        for k in range(nf - 1):
            steps = incoming[k, i].astype(jnp.int32).astype(F32)
            value = steps.reshape(8, span, lanes) * scales[1, k, i][:, None, :]
            preact = preact + value.reshape(chunk, lanes)
        preact = preact + bias_ref[:, cols]
        kept = jnp.where(preact > 0.0, cot_ref[inside(j), cols].astype(F32), 0.0)
        grads[w, at_rows(f, j), :] = kept.astype(BF16)
        for k in range(nf - 1):
            grad_copy(k, i).start()
        hidden_ref[inside(j), cols] = jnp.maximum(preact, 0.0).astype(BF16)

    def others(i):
        for k in range(nf - 1):
            grad_copy(k, i).wait_recv()
            add_grads((f + nf - 1 - k) % nf, i)

    def each(low, high, do):
        def step(i, carry):
            do(i)
            return carry

        if high > low:
            lax.fori_loop(low, high, step, 0)

    started = []

    def reduction(w):
        bias_sum = lax.fori_loop(
            0, nf * chunks, lambda i, acc: acc + sums[w, i], jnp.zeros(sums.shape[2:], F32)
        )
        bias_sum = jnp.broadcast_to(jnp.sum(bias_sum, axis=0, keepdims=True), bias_sum.shape)
        base = 0
        bases = []
        for s, (bit, halve, length) in enumerate(plan):
            partner, side = partners[s]
            bases.append(base)
            if halve:
                keep = base + side * length
                give = base + (1 - side) * length
            else:
                keep = give = base
            keep_rows = pl.ds(pl.multiple_of(keep, 16), length)
            give_rows = pl.ds(pl.multiple_of(give, 16), length)
            small[w, 2 * s] = bias_sum
            staged = len(halves[s]) > 1
            if staged:
                halves[s][1][w] = total[w, give_rows, :].astype(halves[s][1].dtype)
            copy = push(
                halves[s][1].at[w] if staged else total.at[w, give_rows],
                halves[s][0].at[w],
                hsend.at[w, s],
                hrecv.at[w, s],
                "dom",
                partner,
            )
            copy.start()
            tiny = push(
                small.at[w, 2 * s], small.at[w, 2 * s + 1], bsend.at[w, s], brecv.at[w, s], "dom", partner
            )
            tiny.start()
            started.extend((copy, tiny))
            yield
            copy.wait_recv()
            total[w, keep_rows, :] += halves[s][0][w].astype(F32)
            tiny.wait_recv()
            bias_sum = bias_sum + small[w, 2 * s + 1]
            base = keep
        last = plan[-1][2]
        rows = pl.ds(pl.multiple_of(base, 16), last)
        result[w, rows, :] = total[w, rows, :].astype(BF16)
        gb_ref[:, w * lanes : (w + 1) * lanes] = bias_sum
        for s in range(len(plan) - 1, -1, -1):
            bit, halve, length = plan[s]
            if not halve:
                continue
            partner, side = partners[s]
            at = result.at[w, pl.ds(pl.multiple_of(bases[s] + side * length, 16), length)]
            copy = push(at, at, asend.at[w, s], arecv.at[w, s], "dom", partner)
            copy.start()
            started.append(copy)
            yield
            copy.wait_recv()
        gs_ref[:, w * lanes : (w + 1) * lanes] = result[w, 0:width, :]
        gn_ref[:, w * lanes : (w + 1) * lanes] = result[w, width : 2 * width, :]

    def item(i):
        finish(i)

        @pl.when(i + ahead < items)
        def _():
            send_partial(i + ahead)

        add_grads(f, i)

        @pl.when(i >= lag)
        def _():
            others(i - lag)

    each(0, ahead, send_partial)
    running = [reduction(w) for w in range(waves - 1)]
    first = (waves - 1) * chunks + lag if waves > 1 else items
    each(0, first, item)
    for i in range(first, items):
        running = [r for r in running if next(r, 0) is None]
        item(i)
    for i in range(items - lag, items):
        others(i)
        running = [r for r in running if next(r, 0) is None]
    running = [reduction(waves - 1)] + running
    while running:
        running = [r for r in running if next(r, 0) is None]
    for copy in started:
        copy.wait_send()

    def drain(i):
        for k in range(nf - 1):
            scale_copy(k, i).wait_send()
            partial_copy(k, i).wait_send()
            grad_copy(k, i).wait_send()

    each(0, items, drain)


def layer(n, nf, features, aggregated, w_self, w_neigh, hidden_bias, cotangent):
    nodes, width = features.shape
    owned, units = cotangent.shape
    chunk = min(256, owned)
    chunks = owned // chunk
    waves = 2 if units % 256 == 0 else 1
    lanes = units // waves
    items = waves * chunks
    plan = halving_plan(n, 2 * width)
    halves = []
    for bit, halve, length in plan:
        kind = BF16 if halve and bit > 1 else F32
        one = [pltpu.VMEM((waves, length, lanes), kind)]
        if kind == BF16 or not halve:
            one.append(pltpu.VMEM((waves, length, lanes), kind))
        halves.append(tuple(one))
    steps = len(plan)
    dma = pltpu.SemaphoreType.DMA
    others = max(nf - 1, 1)
    return pl.pallas_call(
        functools.partial(layer_kernel, n, nf, plan, chunk, waves),
        out_shape=(
            jax.ShapeDtypeStruct((owned, units), BF16),
            jax.ShapeDtypeStruct((width, units), BF16),
            jax.ShapeDtypeStruct((width, units), BF16),
            jax.ShapeDtypeStruct((8, units), F32),
        ),
        in_specs=[VMEM] * 6,
        out_specs=(VMEM,) * 4,
        scratch_shapes=[
            pltpu.VMEM((others, items, chunk, lanes), jnp.int16),
            pltpu.VMEM((others, items, chunk, lanes), jnp.int16),
            pltpu.VMEM((2, others, items, 8, lanes), F32),
            pltpu.VMEM((waves, nodes, lanes), BF16),
            pltpu.VMEM((waves, 2 * width, lanes), F32),
            pltpu.VMEM((waves, nf * chunks, 8, lanes), F32),
            pltpu.VMEM((waves, 2 * width, lanes), BF16),
            tuple(halves),
            pltpu.VMEM((waves, 2 * steps, 8, lanes), F32),
        ]
        + [dma((others, items))] * 6
        + [dma((waves, steps))] * 6,
        compiler_params=pltpu.CompilerParams(
            collective_id=1, has_side_effects=True, vmem_limit_bytes=28 * 2**20
        ),
    )(features, aggregated, w_self, w_neigh, hidden_bias[None, :], cotangent)


def body(
    n, nf, features, w_self, w_neigh, hidden_bias, edge_tiles, tile_dst, tile_src, tile_count,
    bound_rows, send_pick, cotangent,
):
    source = source_rows(n, features, bound_rows, send_pick[0])
    aggregated = aggregate(
        features.shape[0], source, edge_tiles[0], tile_dst, tile_src, tile_count
    )
    hidden, grad_self, grad_neigh, grad_bias = layer(
        n, nf, features, aggregated, w_self, w_neigh, hidden_bias, cotangent
    )
    return hidden, grad_self, grad_neigh, grad_bias[0]


def solution(mesh):
    placed = (
        P("dom", "feat"),
        P("feat", None),
        P("feat", None),
        P(),
        P("dom", None, None, None),
        P("dom", None),
        P("dom", None),
        P("dom"),
        P("dom", None),
        P("dom", None, None),
        P(("dom", "feat"), None),
    )
    return jax.shard_map(
        functools.partial(body, mesh.shape["dom"], mesh.shape["feat"]),
        mesh=mesh,
        in_specs=placed,
        out_specs=(P(("dom", "feat"), None), P("feat", None), P("feat", None), P()),
        check_vma=False,
    )
```

profile of v0, /device:TPU:0, one launch (start us, length us, event | category | flops | bytes accessed | tf_op | source)
XLA Modules:
  0.0 126.4 jit_solution(4952912365201082749)
XLA Ops:
  1.3 0.7 convert_bitcast_fusion.pick_ref
  2.0 0.0 copy-start
  2.0 2.2 %copy-done = bf16[4096,512]{1,0:T(8,128)(2,1)S(1)} copy-done((bf16[4096,512]{1,0:T(8,128)(2,1)S(1)}, bf16[4096,512]{1,0:T(8,128)(2,1)}, u32[]{:S(2)}) %copy-start) | copy-done | bytes 4194328
  4.2 0.0 copy-start.6
  4.2 0.7 copy-done.6
  4.8 0.0 copy-start.2
  4.8 0.0 copy-start.8
  4.9 0.0 copy-start.9
  4.9 31.4 %shard_map.138.source_ref = bf16[6144,512]{1,0:T(8,128)(2,1)S(1)} custom-call(bf16[4096,512]{1,0:T(8,128)(2,1)S(1)} %copy-done, s32[1,256]{1,0:T(1,128)S(1)} %copy-done.6, bf16[16,128]{1,0:T(8,128)(2,1)S(1)} %convert_bitcast_fusion.pick_ref), custom_call_target="tpu_custom_call" | custom-call | tf_op jit(solution)/shard_map/pallas_call | solution.py:157
  36.2 0.0 copy-done.2
  36.3 0.0 copy-done.8
  36.3 0.0 copy-done.9
  36.3 0.0 copy-start.1
  36.3 0.0 copy-start.3
  36.3 0.0 copy-start.4
  36.3 0.0 copy-start.5
  36.3 0.0 copy-start.7
  36.3 2.5 %shard_map.139.agg_ref = bf16[4096,512]{1,0:T(8,128)(2,1)S(1)} custom-call(s32[1,102]{1,0:T(1,128)S(1)} %copy-done.8, s32[1,102]{1,0:T(1,128)S(1)} %copy-done.9, s32[1]{0:T(128)S(6)} %copy.18.count_ref, bf16[6144,512]{1,0:T(8,128)(2,1)S(1)} %shard_map.138.source_ref, bf16[102,128,128]{2,1,0:T(8,128)(2,1)S(1)} %bitcast.5), custom_call_target="tpu_custom_call" | custom-call | tf_op jit(solution)/shard_map/pallas_call | solution.py:202
  38.8 0.0 copy-done.1
  38.9 0.0 copy-done.3
  38.9 0.0 copy-done.4
  38.9 0.0 copy-done.5
  38.9 0.0 copy-done.7
  38.9 84.6 %shard_map.140 = (bf16[2048,256]{1,0:T(8,128)(2,1)S(1)}, bf16[512,256]{1,0:T(8,128)(2,1)S(1)}, bf16[512,256]{1,0:T(8,128)(2,1)S(1)}, f32[8,256]{1,0:T(8,128)S(1)}) custom-call(bf16[4096,512]{1,0:T(8,128)(2,1)S(1)} %copy-done.1, bf16[4096,512]{1,0:T(8,128)(2,1)S(1)} %shard_map.139.agg_ref, bf16[512,256]{1,0:T(8,128)(2,1)S(1)} %copy-done.4, ...), custom_call_target="tpu_custom_call" | custom-call | tf_op jit(solution)/shard_map/pallas_call | solution.py:471
  123.5 0.6 slice.3
  124.0 1.0 copy.19
  125.0 0.7 copy.20
  125.7 0.7 copy.21
Async XLA Ops:
  2.0 2.2 %copy-start = (bf16[4096,512]{1,0:T(8,128)(2,1)S(1)}, bf16[4096,512]{1,0:T(8,128)(2,1)}, u32[]{:S(2)}) copy-start(bf16[4096,512]{1,0:T(8,128)(2,1)} %feat_ref.3) | copy-start | bytes 12582916
  4.2 0.7 copy-start.6
  4.8 31.4 %copy-start.2 = (bf16[1,102,128,128]{3,2,1,0:T(8,128)(2,1)S(1)}, bf16[1,102,128,128]{3,2,1,0:T(8,128)(2,1)}, u32[]{:S(2)}) copy-start(bf16[1,102,128,128]{3,2,1,0:T(8,128)(2,1)} %param.15) | copy-start | bytes 10027012
  4.8 31.4 %copy-start.8 = (s32[1,102]{1,0:T(1,128)S(1)}, s32[1,102]{1,0:T(1,128)}, u32[]{:S(2)}) copy-start(s32[1,102]{1,0:T(1,128)} %dst_ref.1) | copy-start | bytes 1228
  4.9 31.4 %copy-start.9 = (s32[1,102]{1,0:T(1,128)S(1)}, s32[1,102]{1,0:T(1,128)}, u32[]{:S(2)}) copy-start(s32[1,102]{1,0:T(1,128)} %src_ref.1) | copy-start | bytes 1228
  36.3 2.6 %copy-start.1 = (bf16[4096,512]{1,0:T(8,128)(2,1)S(1)}, bf16[4096,512]{1,0:T(8,128)(2,1)}, u32[]{:S(2)}) copy-start(bf16[4096,512]{1,0:T(8,128)(2,1)} %feat_ref.3) | copy-start | bytes 12582916
  36.3 2.6 %copy-start.3 = (bf16[2048,256]{1,0:T(8,128)(2,1)S(1)}, bf16[2048,256]{1,0:T(8,128)(2,1)}, u32[]{:S(2)}) copy-start(bf16[2048,256]{1,0:T(8,128)(2,1)} %cot_ref.1) | copy-start | bytes 3145732
  36.3 2.6 %copy-start.4 = (bf16[512,256]{1,0:T(8,128)(2,1)S(1)}, bf16[512,256]{1,0:T(8,128)(2,1)}, u32[]{:S(2)}) copy-start(bf16[512,256]{1,0:T(8,128)(2,1)} %ws_ref.1) | copy-start | bytes 786436
  36.3 2.6 %copy-start.5 = (bf16[512,256]{1,0:T(8,128)(2,1)S(1)}, bf16[512,256]{1,0:T(8,128)(2,1)}, u32[]{:S(2)}) copy-start(bf16[512,256]{1,0:T(8,128)(2,1)} %wn_ref.1) | copy-start | bytes 786436
  36.3 2.6 %copy-start.7 = (f32[256]{0:T(256)S(1)}, f32[256]{0:T(256)}, u32[]{:S(2)}) copy-start(f32[256]{0:T(256)} %param.14) | copy-start | bytes 3076
where the time goes:
time: 127 us; the launch traced here: 126 us
  Pallas kernels  118 us (93%)
  local copies, waits for them, and re-layouts  5.85 us (5%)
  between operations  1.41 us (1%)
    pallas_call x1, Pallas kernels, layer(): pl.pallas_call(functools.partial(layer_kernel, n, nf, plan, chunk, waves)...  84.6 us
    pallas_call x1, Pallas kernels, source_rows(): pl.pallas_call(functools.partial(boundary_kernel, n), out_shape=jax.Shape...  31.4 us
    unnamed x23, local copies, waits for them, and re-layouts  5.28 us

commit v1 on v0

--- a/solution.py
+++ b/solution.py
@@ -243,15 +243,19 @@
     for bit, _, _ in plan:
         side = (me // bit) % 2
         partners.append((me + bit - 2 * bit * side, side))
+    joint = len(plan) > 1 and plan[-1][1] and plan[-2][1]
+    reach = [partner for partner, _ in partners]
+    if joint:
+        reach.append(reach[-1] + reach[-2] - me)
     peers = [(f + k) % nf for k in range(1, nf)]
 
     barrier = pltpu.get_barrier_semaphore()
     for peer in peers:
         pl.semaphore_signal(barrier, inc=1, device_id={"feat": peer}, device_id_type=MESH)
-    for partner, _ in partners:
+    for partner in reach:
         pl.semaphore_signal(barrier, inc=1, device_id={"dom": partner}, device_id_type=MESH)
     total[...] = jnp.zeros_like(total)
-    pl.semaphore_wait(barrier, nf - 1 + len(plan))
+    pl.semaphore_wait(barrier, nf - 1 + len(reach))
 
     def at_rows(owner, j):
         return pl.ds(pl.multiple_of(owner * owned + j * chunk, chunk), chunk)
@@ -397,7 +401,18 @@
         rows = pl.ds(pl.multiple_of(base, 16), last)
         result[w, rows, :] = total[w, rows, :].astype(BF16)
         gb_ref[:, w * lanes : (w + 1) * lanes] = bias_sum
-        for s in range(len(plan) - 1, -1, -1):
+        if joint:
+            steps = len(plan)
+            copies = []
+            for slot, partner in ((steps - 1, reach[-2]), (steps - 2, reach[-3]), (steps, reach[-1])):
+                at = result.at[w, rows]
+                copies.append(push(at, at, asend.at[w, slot], arecv.at[w, slot], "dom", partner))
+                copies[-1].start()
+            started.extend(copies)
+            yield
+            for copy in copies:
+                copy.wait_recv()
+        for s in range(len(plan) - (3 if joint else 1), -1, -1):
             bit, halve, length = plan[s]
             if not halve:
                 continue
@@ -490,7 +505,7 @@
             pltpu.VMEM((waves, 2 * steps, 8, lanes), F32),
         ]
         + [dma((others, items))] * 6
-        + [dma((waves, steps))] * 6,
+        + [dma((waves, steps + 1))] * 6,
         compiler_params=pltpu.CompilerParams(
             collective_id=1, has_side_effects=True, vmem_limit_bytes=28 * 2**20
         ),

time: 127 us -> 125 us (0.984)
  Pallas kernels: 118 us -> 116 us
    pallas_call x1, Pallas kernels: 84.6 us -> 81.8 us  [layer(): pl.pallas_call(functools.partial(layer_kernel, n, nf, plan, chunk, waves)...]
where the time goes in v1:
time: 125 us; the launch traced here: 124 us
  Pallas kernels  116 us (93%)
  local copies, waits for them, and re-layouts  5.85 us (5%)
  between operations  1.41 us (1%)
    pallas_call x1, Pallas kernels, layer(): pl.pallas_call(functools.partial(layer_kernel, n, nf, plan, chunk, waves)...  81.8 us
    pallas_call x1, Pallas kernels, source_rows(): pl.pallas_call(functools.partial(boundary_kernel, n), out_shape=jax.Shape...  31.4 us
    unnamed x23, local copies, waits for them, and re-layouts  5.28 us
    pallas_call x1, Pallas kernels, aggregate(): pl.pallas_call(functools.partial(tile_kernel, group), out_shape=jax.Shape...  2.5 us

profile of v1, /device:TPU:0, one launch (start us, length us, event | category | flops | bytes accessed | tf_op | source)
XLA Modules:
  0.0 123.6 jit_solution(2079540649008106400)
XLA Ops:
  1.3 0.7 convert_bitcast_fusion.pick_ref
  2.0 0.0 copy-start
  2.0 2.2 %copy-done = bf16[4096,512]{1,0:T(8,128)(2,1)S(1)} copy-done((bf16[4096,512]{1,0:T(8,128)(2,1)S(1)}, bf16[4096,512]{1,0:T(8,128)(2,1)}, u32[]{:S(2)}) %copy-start) | copy-done | bytes 4194328
  4.2 0.0 copy-start.6
  4.2 0.7 copy-done.6
  4.8 0.0 copy-start.2
  4.8 0.0 copy-start.8
  4.9 0.0 copy-start.9
  4.9 31.4 %shard_map.138.source_ref = bf16[6144,512]{1,0:T(8,128)(2,1)S(1)} custom-call(bf16[4096,512]{1,0:T(8,128)(2,1)S(1)} %copy-done, s32[1,256]{1,0:T(1,128)S(1)} %copy-done.6, bf16[16,128]{1,0:T(8,128)(2,1)S(1)} %convert_bitcast_fusion.pick_ref), custom_call_target="tpu_custom_call" | custom-call | tf_op jit(solution)/shard_map/pallas_call | solution.py:157
  36.2 0.0 copy-done.2
  36.3 0.0 copy-done.8
  36.3 0.0 copy-done.9
  36.3 0.0 copy-start.1
  36.3 0.0 copy-start.3
  36.3 0.0 copy-start.4
  36.3 0.0 copy-start.5
  36.3 0.0 copy-start.7
  36.3 2.5 %shard_map.139.agg_ref = bf16[4096,512]{1,0:T(8,128)(2,1)S(1)} custom-call(s32[1,102]{1,0:T(1,128)S(1)} %copy-done.8, s32[1,102]{1,0:T(1,128)S(1)} %copy-done.9, s32[1]{0:T(128)S(6)} %copy.18.count_ref, bf16[6144,512]{1,0:T(8,128)(2,1)S(1)} %shard_map.138.source_ref, bf16[102,128,128]{2,1,0:T(8,128)(2,1)S(1)} %bitcast.5), custom_call_target="tpu_custom_call" | custom-call | tf_op jit(solution)/shard_map/pallas_call | solution.py:202
  38.8 0.0 copy-done.1
  38.9 0.0 copy-done.3
  38.9 0.0 copy-done.4
  38.9 0.0 copy-done.5
  38.9 0.0 copy-done.7
  38.9 81.8 %shard_map.140 = (bf16[2048,256]{1,0:T(8,128)(2,1)S(1)}, bf16[512,256]{1,0:T(8,128)(2,1)S(1)}, bf16[512,256]{1,0:T(8,128)(2,1)S(1)}, f32[8,256]{1,0:T(8,128)S(1)}) custom-call(bf16[4096,512]{1,0:T(8,128)(2,1)S(1)} %copy-done.1, bf16[4096,512]{1,0:T(8,128)(2,1)S(1)} %shard_map.139.agg_ref, bf16[512,256]{1,0:T(8,128)(2,1)S(1)} %copy-done.4, ...), custom_call_target="tpu_custom_call" | custom-call | tf_op jit(solution)/shard_map/pallas_call | solution.py:486
  120.7 0.6 slice.3
  121.2 1.0 copy.19
  122.2 0.7 copy.20
  122.9 0.7 copy.21
Async XLA Ops:
  2.0 2.2 %copy-start = (bf16[4096,512]{1,0:T(8,128)(2,1)S(1)}, bf16[4096,512]{1,0:T(8,128)(2,1)}, u32[]{:S(2)}) copy-start(bf16[4096,512]{1,0:T(8,128)(2,1)} %feat_ref.3) | copy-start | bytes 12582916
  4.2 0.7 copy-start.6
  4.8 31.4 %copy-start.2 = (bf16[1,102,128,128]{3,2,1,0:T(8,128)(2,1)S(1)}, bf16[1,102,128,128]{3,2,1,0:T(8,128)(2,1)}, u32[]{:S(2)}) copy-start(bf16[1,102,128,128]{3,2,1,0:T(8,128)(2,1)} %param.15) | copy-start | bytes 10027012
  4.8 31.4 %copy-start.8 = (s32[1,102]{1,0:T(1,128)S(1)}, s32[1,102]{1,0:T(1,128)}, u32[]{:S(2)}) copy-start(s32[1,102]{1,0:T(1,128)} %dst_ref.1) | copy-start | bytes 1228
  4.9 31.4 %copy-start.9 = (s32[1,102]{1,0:T(1,128)S(1)}, s32[1,102]{1,0:T(1,128)}, u32[]{:S(2)}) copy-start(s32[1,102]{1,0:T(1,128)} %src_ref.1) | copy-start | bytes 1228
  36.3 2.6 %copy-start.1 = (bf16[4096,512]{1,0:T(8,128)(2,1)S(1)}, bf16[4096,512]{1,0:T(8,128)(2,1)}, u32[]{:S(2)}) copy-start(bf16[4096,512]{1,0:T(8,128)(2,1)} %feat_ref.3) | copy-start | bytes 12582916
  36.3 2.6 %copy-start.3 = (bf16[2048,256]{1,0:T(8,128)(2,1)S(1)}, bf16[2048,256]{1,0:T(8,128)(2,1)}, u32[]{:S(2)}) copy-start(bf16[2048,256]{1,0:T(8,128)(2,1)} %cot_ref.1) | copy-start | bytes 3145732
  36.3 2.6 %copy-start.4 = (bf16[512,256]{1,0:T(8,128)(2,1)S(1)}, bf16[512,256]{1,0:T(8,128)(2,1)}, u32[]{:S(2)}) copy-start(bf16[512,256]{1,0:T(8,128)(2,1)} %ws_ref.1) | copy-start | bytes 786436
  36.3 2.6 %copy-start.5 = (bf16[512,256]{1,0:T(8,128)(2,1)S(1)}, bf16[512,256]{1,0:T(8,128)(2,1)}, u32[]{:S(2)}) copy-start(bf16[512,256]{1,0:T(8,128)(2,1)} %wn_ref.1) | copy-start | bytes 786436
  36.3 2.6 %copy-start.7 = (f32[256]{0:T(256)S(1)}, f32[256]{0:T(256)}, u32[]{:S(2)}) copy-start(f32[256]{0:T(256)} %param.14) | copy-start | bytes 3076
